TPU v7x, 256 devices: a whole 4x4x8 slice. The times are simulated.
256 devices in a mesh: region: 8 (over z), owner: 32 (over x, y, core).
Axes of the slice: x: 4, y: 4, z: 8, core: 2. Of those that a mesh axis runs over, the one named last changes fastest.
Arguments:
- features: bfloat16 [1024, 64, 1728], P(('region', 'owner')), may hold values from -6 to 6
- conv_weight: bfloat16 [27, 64, 64], replicated, may hold values from -0.15625 to 0.15625
- down_weight: bfloat16 [8, 128, 64], replicated, may hold values from -0.25 to 0.25
- fine_grad: bfloat16 [1024, 64, 1728], P(('region', 'owner')), may hold values from -6 to 6
- coarse_grad: bfloat16 [256, 128, 8, 216], P(('region', 'owner')), may hold values from -6 to 6
- face_send: int32 [256, 2, 4, 2], P(('region', 'owner')), may hold values from 0 to 7, as said below
- face_recv: int32 [1024, 2, 2], P(('region', 'owner')), may hold values from 8 to 15, as said below
- z_recv: int32 [1024, 2], P(('region', 'owner')), may hold values from 0 to 8, as said below
- parent_send: int32 [256, 4], P(('region', 'owner')), may hold values from 0 to 3, as said below
- parent_recv: int32 [256, 8], P(('region', 'owner')), may hold values from 0 to 4, as said below
Outputs:
- fine_out: bfloat16 [1024, 64, 1728], P(('region', 'owner'))
- coarse_out: bfloat16 [256, 128, 8, 216], P(('region', 'owner'))
- grad_in: bfloat16 [1024, 64, 1728], P(('region', 'owner'))
- grad_conv: float32 [27, 64, 64], replicated
- grad_down: float32 [8, 128, 64], replicated
Inputs may be any that keep to these rules, and one draw needn't show every extreme that they name: `face_send`: entry [d, m, s] names one of the device's own faces of round d; each of its 8 faces is named exactly once in each round. `face_recv`: every entry names a received face. `z_recv`: 8 names the zero face; the lowest region's entry 0 and the highest region's entry 1 are always it. `parent_send`: each row is a permutation of the device's slots. `parent_recv`: entry q is a distance index or 4 for an empty octant; each distance index is named exactly once in a row.
All inputs are finite; a program needn't handle non-finite values.
Results may differ from a plain program's by a relative error of at most 0.005.
Values may be sent and summed in bfloat16 or wider, within the bound.
A program may use at most 64 MiB of HBM per device.

v0:
```python
import math

import jax
import jax.numpy as jnp
import numpy as np
from jax import lax
from jax.experimental import pallas as pl
from jax.experimental.pallas import tpu as pltpu
from jax.sharding import PartitionSpec as P


C = 64
C2 = 128
VOX = 1728
B = 4
PROWS = 14 * 7 * 8
ROWS = 6 * 6 * 16
TAPS = 12
OFFSETS = (1, -1, 2, -2)
N_OWNER = 32
N_REGION = 8
CHUNK = 48
GROWS = N_OWNER * CHUNK
BF = jnp.bfloat16
F32 = jnp.float32
MESH = pl.DeviceIdType.MESH
VMEM_LIMIT = 56 * 1024 * 1024


def select_in(padded):
    count = 7 if padded else 6
    back = 1 if padded else 0
    out = np.zeros((8, 4, count * 8, 256), np.float32)
    for v in range(8):
        for e in range(2):
            for f in range(2):
                for jj in range(count):
                    for ll in range(count):
                        j, l = 2 * jj + e - back, 2 * ll + f - back
                        if 0 <= j < 12 and 0 <= l < 12:
                            col = 16 * v + j * 12 + l
                            if col < 256:
                                out[v, 2 * e + f, jj * 8 + ll, col] = 1
    return out.reshape(8, 4 * count * 8, 256).astype(BF)


def select_out():
    out = np.zeros((2, 2, 128, 288), np.float32)
    for e in range(2):
        for f in range(2):
            for jj in range(6):
                for s in range(2):
                    for ll in range(6):
                        out[e, f, jj * 16 + s * 8 + ll, s * 144 + (2 * jj + e) * 12 + 2 * ll + f] = 1
    return out.reshape(2, 256, 288).astype(BF)


def coarse_selects():
    down = np.zeros((768, 216), np.float32)
    up = np.zeros((288, 216), np.float32)
    spread = np.zeros((216, 2 * ROWS), np.float32)
    for ii in range(6):
        for jj in range(6):
            for ll in range(6):
                cell = ii * 36 + jj * 6 + ll
                down[ii * 128 + jj * 16 + ll, cell] = 1
                up[(ii * 6 + jj) * 8 + ll, cell] = 1
                for s in range(2):
                    spread[cell, s * ROWS + (ii * 6 + jj) * 16 + s * 8 + ll] = 1
    return down.astype(BF), up.astype(BF), spread.astype(BF)


def octant_swap():
    out = np.zeros((256, 256), np.float32)
    for q in range(8):
        for c in range(32):
            out[q * 32 + c, c * 8 + q] = 1
    return out.astype(BF)


def dot(a, b):
    return jnp.dot(a, b, preferred_element_type=F32)


def dot_t(a, b):
    return lax.dot_general(a, b, (((1,), (1,)), ((), ())), preferred_element_type=F32)


def low_lanes(rows):
    return lax.broadcasted_iota(jnp.int32, (rows, 128), 1) < 64


def to_rows(src_ref, sel_ref, count, put):
    nr = count * 8
    low = low_lanes(nr)
    for i in range(12):
        start = (144 * i) // 128 * 128
        width = min(256, VOX - start)
        window = src_ref[:, :, start : start + width].reshape(B * C, width)
        rows = dot_t(sel_ref[i % 8, :, :width], window)
        for e in range(2):
            for pair in range(2):
                lanes = slice(pair * 128, pair * 128 + 128)
                first = rows[2 * e * nr : (2 * e + 1) * nr, lanes]
                second = rows[(2 * e + 1) * nr : (2 * e + 2) * nr, lanes]
                put(2 * pair, i, e, jnp.where(low, first, pltpu.roll(second, 64, 1)))
                put(2 * pair + 1, i, e, jnp.where(low, pltpu.roll(first, 64, 1), second))


def from_rows(turned, sel_ref):
    total = None
    for e in range(2):
        blocks = [
            jnp.concatenate(
                [turned[(2 * e + f) * 64 : (2 * e + f + 1) * 64, ii * 128 : ii * 128 + 128] for f in range(2)], axis=1
            )
            for ii in range(6)
        ]
        part = dot(jnp.concatenate(blocks, axis=0), sel_ref[e])
        total = part if total is None else total + part
    return jnp.concatenate([total[ii * 64 : ii * 64 + 64] for ii in range(6)], axis=1)


def im2col(pad_ref, b, put):
    def step(ii, carry):
        for e in range(2):
            slabs = pad_ref[b, e, pl.ds(pl.multiple_of(ii * 112, 8), 224), :]
            shifted = pltpu.roll(slabs, 223, 0)
            for a in range(3):
                for dj in range(2):
                    for dl, source in ((0, slabs), (1, shifted)):
                        pieces = []
                        for jj in range(6):
                            for s in range(2):
                                row = ((a + s) * 7 + jj + dj) * 8
                                pieces.append(source[row : row + 8])
                        put(ii, ((a * 2 + dj) * 2 + dl) * 2 + e, jnp.concatenate(pieces, axis=0).astype(BF))
        return carry

    lax.fori_loop(0, 6, step, 0)


class Rounds:
    def __init__(self, pad, send_list, recv_list, z_list, bufs):
        self.pad, self.send_list, self.recv_list, self.z_list = pad, send_list, recv_list, z_list
        (self.sx, self.rx, self.sy, self.ry, self.sz, self.rz, self.ssem, self.rsem) = bufs
        self.region = lax.axis_index("region")
        self.owner = lax.axis_index("owner")

    def owner_copies(self, send, recv, base):
        out = []
        for m, t in enumerate(OFFSETS):
            out.append(
                pltpu.make_async_remote_copy(
                    src_ref=send.at[pl.ds(2 * m, 2)],
                    dst_ref=recv.at[pl.ds(2 * m, 2)],
                    send_sem=self.ssem.at[base + m],
                    recv_sem=self.rsem.at[base + m],
                    device_id=(self.region, lax.rem(self.owner + (t + N_OWNER), N_OWNER)),
                    device_id_type=MESH,
                )
            )
        return out

    def x_copies(self):
        return self.owner_copies(self.sx, self.rx, 0)

    def y_copies(self):
        return self.owner_copies(self.sy, self.ry, 4)

    def z_copies(self):
        out = []
        for m, t in enumerate((1, N_REGION - 1)):
            out.append(
                pltpu.make_async_remote_copy(
                    src_ref=self.sz.at[pl.ds(4 * m, 4)],
                    dst_ref=self.rz.at[pl.ds(4 * m, 4)],
                    send_sem=self.ssem.at[8 + m],
                    recv_sem=self.rsem.at[8 + m],
                    device_id=(lax.rem(self.region + t, N_REGION), self.owner),
                    device_id_type=MESH,
                )
            )
        return out

    def x_start(self):
        for n in range(8):
            pick = self.send_list[0, 0, n // 2, n % 2]
            slot, high = lax.rem(pick, 4), pick >= 4
            for e in range(2):
                low_face = self.pad[slot, e, 56:112, :]
                high_face = self.pad[slot, e, 672:728, :]
                self.sx[n, :, e * 128 : e * 128 + 128] = jnp.where(high, high_face, low_face).astype(BF)
        for copy in self.x_copies():
            copy.start()

    def x_end(self):
        for copy in self.x_copies():
            copy.wait_recv()
        for b in range(B):
            low_pad = self.rx[jnp.maximum(self.recv_list[b, 0, 0] - 8, 0)].astype(F32)
            high_pad = self.rx[jnp.maximum(self.recv_list[b, 0, 1] - 8, 0)].astype(F32)
            for e in range(2):
                self.pad[b, e, 0:56, :] = low_pad[:, e * 128 : e * 128 + 128]
                self.pad[b, e, 728:784, :] = high_pad[:, e * 128 : e * 128 + 128]

    def y_start(self):
        for n in range(8):
            pick = self.send_list[0, 1, n // 2, n % 2]
            slot, high = lax.rem(pick, 4), pick >= 4
            faces = []
            for i in range(14):
                low_face = self.pad[slot, 1, i * 56 : i * 56 + 8, :]
                high_face = self.pad[slot, 0, i * 56 + 48 : i * 56 + 56, :]
                faces.append(jnp.where(high, high_face, low_face))
            self.sy[n] = jnp.concatenate(faces, axis=0).astype(BF)
        for copy in self.y_copies():
            copy.start()

    def y_end(self):
        for copy in self.y_copies():
            copy.wait_recv()
        for b in range(B):
            low_pad = self.ry[jnp.maximum(self.recv_list[b, 1, 0] - 8, 0)].astype(F32)
            high_pad = self.ry[jnp.maximum(self.recv_list[b, 1, 1] - 8, 0)].astype(F32)
            for i in range(14):
                self.pad[b, 0, i * 56 : i * 56 + 8, :] = low_pad[i * 8 : i * 8 + 8]
                self.pad[b, 1, i * 56 + 48 : i * 56 + 56, :] = high_pad[i * 8 : i * 8 + 8]

    def z_start(self):
        low = low_lanes(98)
        for b in range(B):
            tiles = [self.pad[b, e, pl.ds(6, 98, stride=8), :] for e in range(2)]
            self.sz[b] = jnp.where(low, tiles[0], pltpu.roll(tiles[1], 64, 1)).astype(BF)
            tiles = [self.pad[b, e, pl.ds(0, 98, stride=8), :] for e in range(2)]
            self.sz[4 + b] = jnp.where(low, pltpu.roll(tiles[0], 64, 1), tiles[1]).astype(BF)
        for copy in self.z_copies():
            copy.start()

    def z_end(self):
        for copy in self.z_copies():
            copy.wait_recv()
        low = low_lanes(98)
        for b in range(B):
            for side in range(2):
                pick = self.z_list[b, side]
                zero = (pick == 8) | ((pick < 4) & (self.region == 0)) | ((pick >= 4) & (self.region == N_REGION - 1))
                face = self.rz[jnp.minimum(pick, 7)].astype(F32)
                face = jnp.where(zero, jnp.zeros_like(face), face)
                turned = pltpu.roll(face, 64, 1)
                row = 6 * side
                for e in range(2):
                    at = (b, e, pl.ds(row, 98, stride=8))
                    tile = self.pad[at]
                    if side == 0:
                        self.pad[at] = jnp.where(low, turned if e else face, tile)
                    else:
                        self.pad[at] = jnp.where(low, tile, face if e else turned)

    def drain(self):
        for copy in self.x_copies() + self.y_copies() + self.z_copies():
            copy.wait_send()


def round_scratch():
    return [
        pltpu.VMEM((8, 56, 256), BF),
        pltpu.VMEM((8, 56, 256), BF),
        pltpu.VMEM((8, 112, 128), BF),
        pltpu.VMEM((8, 112, 128), BF),
        pltpu.VMEM((8, 98, 128), BF),
        pltpu.VMEM((8, 98, 128), BF),
        pltpu.SemaphoreType.DMA((10,)),
        pltpu.SemaphoreType.DMA((10,)),
    ]


def meet(owners, regions):
    region, owner = lax.axis_index("region"), lax.axis_index("owner")
    barrier = pltpu.get_barrier_semaphore()
    for t in owners:
        pl.semaphore_signal(
            barrier, inc=1, device_id=(region, lax.rem(owner + (t + N_OWNER), N_OWNER)), device_id_type=MESH
        )
    for t in regions:
        pl.semaphore_signal(
            barrier, inc=1, device_id=(lax.rem(region + (t + N_REGION), N_REGION), owner), device_id_type=MESH
        )
    pl.semaphore_wait(barrier, len(owners) + len(regions))


def meet_all():
    region, owner = lax.axis_index("region"), lax.axis_index("owner")
    barrier = pltpu.get_barrier_semaphore()

    def one_owner(d, carry):
        pl.semaphore_signal(barrier, inc=1, device_id=(region, lax.rem(owner + d, N_OWNER)), device_id_type=MESH)
        return carry

    def one_region(d, carry):
        pl.semaphore_signal(barrier, inc=1, device_id=(lax.rem(region + d, N_REGION), owner), device_id_type=MESH)
        return carry

    lax.fori_loop(1, N_OWNER, one_owner, 0)
    lax.fori_loop(1, N_REGION, one_region, 0)
    pl.semaphore_wait(barrier, N_OWNER + N_REGION - 2)


def gather_kernel(
    feat, coarse, send_list, recv_list, z_list, p_send, p_recv, sel_in, swap, pad, child, octs, csend, crecv, cs, cr, *bufs
):
    region, owner = lax.axis_index("region"), lax.axis_index("owner")
    meet((1, -1, 2, -2, 3, -3, 4, -4), (1, -1))
    rounds = Rounds(pad, send_list, recv_list, z_list, bufs)

    def put(b, i, e, value):
        pad[b, e, (i + 1) * 56 : (i + 2) * 56, :] = value

    to_rows(feat, sel_in, 7, put)
    rounds.x_start()
    for g in range(4):
        rows = dot(swap[...], coarse[g * 256 : g * 256 + 256, :]).astype(BF)
        for q in range(8):
            octs[q, g * 32 : g * 32 + 32, :] = rows[q * 32 : q * 32 + 32]
    copies = []
    for m in range(4):
        index = jnp.int32(0)
        for q in range(8):
            index = jnp.where(p_recv[0, q] == m, q, index)
        csend[m] = octs[index]
        copies.append(
            pltpu.make_async_remote_copy(
                src_ref=csend.at[m],
                dst_ref=crecv.at[m],
                send_sem=cs.at[m],
                recv_sem=cr.at[m],
                device_id=(region, lax.rem(owner + (N_OWNER - m - 1), N_OWNER)),
                device_id_type=MESH,
            )
        )
    for copy in copies:
        copy.start()
    rounds.x_end()
    rounds.y_start()
    rounds.y_end()
    rounds.z_start()
    for copy in copies:
        copy.wait_recv()
    for k in range(B):
        index = jnp.int32(0)
        for m in range(4):
            index = jnp.where(p_send[0, m] == k, m, index)
        child[k] = crecv[index]
    rounds.z_end()
    rounds.drain()
    for copy in copies:
        copy.wait_send()


def compute_kernel(
    pad, fgrad, child, weight, down, sel_fg, sel_out, sel_down, sel_up, sel_spread, eye,
    fine, contrib, pre, grads,
    cols, wide, lhs, fg, fine8, turned, spread, fine_rows,
):
    zero = jnp.zeros((64, 64), BF)
    for e1 in range(2):
        for f1 in range(2):
            for a in range(3):
                for dj in range(2):
                    for dl in range(2):
                        for e in range(2):
                            te = 2 * dj + e - e1
                            blocks = []
                            for f in range(2):
                                tf = 2 * dl + f - f1
                                ok = 0 <= te < 3 and 0 <= tf < 3
                                blocks.append(weight[9 * a + 3 * te + tf] if ok else zero)
                            lane = ((a * 2 + dj) * 2 + dl) * 256 + e * 128
                            row = (2 * e1 + f1) * 64
                            wide[row : row + 64, lane : lane + 128] = jnp.concatenate(blocks, axis=1)
    lhs[0:256, :] = eye[...]
    for s in range(2):
        for e in range(2):
            pair = [down[4 * s + 2 * e + f] for f in range(2)]
            lhs[256 + s * 128 : 384 + s * 128, e * 128 : e * 128 + 128] = jnp.concatenate(pair, axis=1)

    def put_grad(b, i, e, value):
        for jj in range(6):
            row = ((i // 2) * 6 + jj) * 16 + (i % 2) * 8
            fg[b, row : row + 8, e * 128 : e * 128 + 128] = value[jj * 8 : jj * 8 + 8]

    to_rows(fgrad, sel_fg, 6, put_grad)
    for ii in range(6):
        fine8[ii * 128 + 96 : ii * 128 + 128, :] = jnp.zeros((32, 256), BF)
    live = lax.rem(lax.broadcasted_iota(jnp.int32, (ROWS, 256), 0), 8) < 6

    def brick(b, carry):
        base = pl.multiple_of(b * ROWS, 16)

        def put(ii, k, value):
            cols[pl.ds(pl.multiple_of(base + ii * 96, 16), 96), k * 128 : k * 128 + 128] = value

        im2col(pad, b, put)
        act = dot_t(cols[pl.ds(base, ROWS), :], wide[...])
        sig = 1.0 / (1.0 + jnp.exp(-act))
        rows = (act * sig).astype(BF)
        fine_rows[pl.ds(base, ROWS), :] = rows
        for ii in range(6):
            fine8[ii * 128 : ii * 128 + 96, :] = rows[ii * 96 : ii * 96 + 96]
        slope = sig * (1.0 + act * (1.0 - sig))
        kid = child[b]
        up_rows = dot_t(sel_up[...], kid).astype(BF)
        halves = [dot(up_rows, lhs[256 + s * 128 : 384 + s * 128, :]) for s in range(2)]
        pieces = []
        for t in range(36):
            for s in range(2):
                pieces.append(halves[s][t * 8 : t * 8 + 8])
        grad = (fg[b] + jnp.concatenate(pieces, axis=0)) * slope
        grad = jnp.where(live, grad, 0.0).astype(BF)
        pre[b] = grad
        turned[b] = dot_t(lhs[0:256, :], grad).astype(BF)
        for s in range(2):
            spread[b, s * 128 : s * 128 + 128, :] = dot(kid, sel_spread[:, s * ROWS : (s + 1) * ROWS]).astype(BF)
        both = dot_t(lhs[...], fine8[...])
        fine[b] = from_rows(both[0:256].astype(BF), sel_out).astype(BF)
        sums = both[256:384] + pltpu.roll(both[384:512], 760, 1)
        contrib[b] = dot(sums.astype(BF), sel_down[...]).astype(BF)
        return carry

    lax.fori_loop(0, B, brick, 0)

    low = low_lanes(64)
    main = [[None] * 3 for _ in range(3)]
    last = [[None] * 3 for _ in range(3)]

    def add(total, value):
        return value if total is None else total + value

    for a in range(3):
        for dj in range(2):
            tiles = []
            for dl in range(2):
                k = (a * 2 + dj) * 2 + dl
                total = None
                for b in range(B):
                    total = add(total, dot(turned[b], cols[b * ROWS : (b + 1) * ROWS, k * 256 : k * 256 + 256]))
                tiles.append(total)
            for e1 in range(2):
                for e in range(2):
                    te = 2 * dj + e - e1
                    if not 0 <= te < 3:
                        continue
                    lanes = slice(e * 128, e * 128 + 128)
                    t0, t1 = (tiles[dl][e1 * 128 : e1 * 128 + 64, lanes] for dl in range(2))
                    main[a][te] = add(main[a][te], t0)
                    last[a][te] = add(last[a][te], t1)
                    t0, t1 = (pltpu.roll(tiles[dl][e1 * 128 + 64 : e1 * 128 + 128, lanes], 64, 1) for dl in range(2))
                    main[a][te] = add(main[a][te], jnp.where(low, t0, t1))
                    last[a][te] = add(last[a][te], t1)
    main = main[0] + main[1] + main[2]
    last = last[0] + last[1] + last[2]
    for n in range(9):
        grads[n * 64 : n * 64 + 64, :] = main[n]
    for n in range(5):
        other = pltpu.roll(last[2 * n + 1], 64, 1) if n < 4 else jnp.zeros((64, 128), F32)
        grads[576 + n * 64 : 640 + n * 64, :] = jnp.where(low, last[2 * n], other)
    total = None
    for b in range(B):
        total = add(total, dot(spread[b], fine_rows[b * ROWS : (b + 1) * ROWS, :]))
    for e in range(2):
        grads[896 + e * 256 : 1152 + e * 256, :] = total[:, e * 128 : e * 128 + 128]
    grads[1408:1536, :] = jnp.zeros((128, 128), F32)


def reduce_kernel(
    pre, contrib, grads, send_list, recv_list, z_list, p_send, p_recv, swap,
    pad_out, coarse, conv_out, down_out,
    pad, csend, crecv, cs, cr, first, second, third, s1, r1, s2, r2, s3, r3, *bufs,
):
    region, owner = lax.axis_index("region"), lax.axis_index("owner")
    meet_all()
    rounds = Rounds(pad, send_list, recv_list, z_list, bufs)

    def leg1(d):
        to = lax.rem(owner + d, N_OWNER)
        return pltpu.make_async_remote_copy(
            src_ref=grads.at[to], dst_ref=first.at[d], send_sem=s1.at[d], recv_sem=r1.at[d],
            device_id=(region, to), device_id_type=MESH,
        )

    def leg2(d):
        return pltpu.make_async_remote_copy(
            src_ref=second.at[region], dst_ref=second.at[region], send_sem=s2.at[d], recv_sem=r2.at[d],
            device_id=(lax.rem(region + d, N_REGION), owner), device_id_type=MESH,
        )

    def leg3(d):
        return pltpu.make_async_remote_copy(
            src_ref=third.at[owner], dst_ref=third.at[owner], send_sem=s3.at[d], recv_sem=r3.at[d],
            device_id=(region, lax.rem(owner + d, N_OWNER)), device_id_type=MESH,
        )

    def each(count, leg, what):
        def body(d, carry):
            getattr(leg(d), what)()
            return carry

        lax.fori_loop(1, count, body, 0)

    low = low_lanes(48)
    edge = jnp.zeros((8, 128), F32)
    for b in range(B):
        for e in range(2):
            pad[b, e, 0:56, :] = jnp.zeros((56, 128), F32)
            pad[b, e, 728:784, :] = jnp.zeros((56, 128), F32)
    for b in range(B):

        def slab(ii, carry):
            rows = pre[b, pl.ds(pl.multiple_of(ii * 96, 16), 96), :].astype(F32)
            for s in range(2):
                to = pl.multiple_of((2 * ii + s + 1) * 56, 8)
                for e in range(2):
                    tile = jnp.concatenate(
                        [rows[jj * 16 + s * 8 : jj * 16 + s * 8 + 8, e * 128 : e * 128 + 128] for jj in range(6)], axis=0
                    )
                    tile = pltpu.roll(tile, 64, 1)
                    tile = jnp.where(low, pltpu.roll(tile, 1, 0), tile)
                    if e == 0:
                        pad[b, 1, pl.ds(to, 48), :] = tile
                        pad[b, 1, pl.ds(to + 48, 8), :] = edge
                    else:
                        pad[b, 0, pl.ds(to + 8, 48), :] = tile
                        pad[b, 0, pl.ds(to, 8), :] = edge
            return carry

        lax.fori_loop(0, 6, slab, 0)
    rounds.x_start()
    copies = []
    for m in range(4):
        csend[m] = contrib[p_send[0, m]]
        copies.append(
            pltpu.make_async_remote_copy(
                src_ref=csend.at[m], dst_ref=crecv.at[m], send_sem=cs.at[m], recv_sem=cr.at[m],
                device_id=(region, lax.rem(owner + (m + 1), N_OWNER)), device_id_type=MESH,
            )
        )
    for copy in copies:
        copy.start()
    each(N_OWNER, leg1, "start")
    rounds.x_end()
    rounds.y_start()
    rounds.y_end()
    rounds.z_start()
    for copy in copies:
        copy.wait_recv()
    crecv[4] = jnp.zeros((C2, 216), BF)
    parts = [crecv[p_recv[0, q]] for q in range(8)]
    for g in range(4):
        rows = jnp.concatenate([part[g * 32 : g * 32 + 32] for part in parts], axis=0)
        turned = lax.dot_general(swap[...], rows, (((0,), (0,)), ((), ())), preferred_element_type=F32)
        coarse[g * 256 : g * 256 + 256, :] = turned.astype(BF)
    rounds.z_end()
    pad_out[...] = pad[...]

    each(N_OWNER, leg1, "wait_recv")
    second[region] = lax.fori_loop(1, N_OWNER, lambda d, total: total + first[d], grads[owner])
    each(N_REGION, leg2, "start")
    each(N_REGION, leg2, "wait_recv")
    third[owner] = lax.fori_loop(1, N_REGION, lambda d, total: total + second[d], second[0])
    each(N_OWNER, leg3, "start")
    each(N_OWNER, leg3, "wait_recv")
    factor = 1.0 / math.sqrt(B * N_OWNER * N_REGION * VOX)
    total = third[...].reshape(GROWS, 128) * factor
    for n in range(9):
        tile = total[n * 64 : n * 64 + 64]
        conv_out[3 * n] = tile[:, 0:64]
        conv_out[3 * n + 1] = tile[:, 64:128]
        row = 576 + (n // 2) * 64
        conv_out[3 * n + 2] = total[row : row + 64, (n % 2) * 64 : (n % 2) * 64 + 64]
    for s in range(2):
        for e in range(2):
            row = 896 + e * 256 + s * 128
            for f in range(2):
                down_out[4 * s + 2 * e + f] = total[row : row + 128, f * 64 : f * 64 + 64]
    rounds.drain()
    for copy in copies:
        copy.wait_send()
    each(N_OWNER, leg1, "wait_send")
    each(N_REGION, leg2, "wait_send")
    each(N_OWNER, leg3, "wait_send")


def back_kernel(pad, weight, sel_out, eye, grad_in, cols, tall, rows8):
    zero = jnp.zeros((64, 64), BF)
    for e1 in range(2):
        for a in range(3):
            for dj in range(2):
                for dl in range(2):
                    for e in range(2):
                        te = 2 * dj + e - e1
                        for f in range(2):
                            blocks = []
                            for f1 in range(2):
                                tf = 2 * dl + f - f1
                                ok = 0 <= te < 3 and 0 <= tf < 3
                                blocks.append(weight[9 * (2 - a) + 3 * (2 - te) + 2 - tf] if ok else zero)
                            row = ((a * 2 + dj) * 2 + dl) * 256 + (2 * e + f) * 64
                            tall[row : row + 64, e1 * 128 : e1 * 128 + 128] = jnp.concatenate(blocks, axis=1)
    for ii in range(6):
        rows8[ii * 128 + 96 : ii * 128 + 128, :] = jnp.zeros((32, 256), BF)

    def brick(b, carry):
        def put(ii, k, value):
            cols[pl.ds(pl.multiple_of(ii * 96, 16), 96), k * 128 : k * 128 + 128] = value

        im2col(pad, b, put)
        rows = dot(cols[...], tall[...]).astype(BF)
        for ii in range(6):
            rows8[ii * 128 : ii * 128 + 96, :] = rows[ii * 96 : ii * 96 + 96]
        grad_in[b] = from_rows(dot_t(eye[...], rows8[...]).astype(BF), sel_out).astype(BF)
        return carry

    lax.fori_loop(0, B, brick, 0)


VM = pl.BlockSpec(memory_space=pltpu.VMEM)
SM = pl.BlockSpec(memory_space=pltpu.SMEM)


def struct(shape, kind):
    return jax.ShapeDtypeStruct(shape, kind)


def local(
    features, conv_weight, down_weight, fine_grad, coarse_grad, face_send, face_recv, z_recv, parent_send, parent_recv
):
    sel_down, sel_up, sel_spread = coarse_selects()
    swap = jnp.asarray(octant_swap())
    eye = jnp.asarray(np.eye(256, dtype=np.float32).astype(BF))
    sel_out = jnp.asarray(select_out())
    lists = (face_send, face_recv, z_recv, parent_send, parent_recv)
    pad, child = pl.pallas_call(
        gather_kernel,
        out_shape=(struct((B, 2, PROWS, 128), F32), struct((B, C2, 216), BF)),
        in_specs=[VM, VM] + [SM] * 5 + [VM, VM],
        out_specs=(VM, VM),
        scratch_shapes=[
            pltpu.VMEM((8, C2, 216), BF),
            pltpu.VMEM((4, C2, 216), BF),
            pltpu.VMEM((4, C2, 216), BF),
            pltpu.SemaphoreType.DMA((4,)),
            pltpu.SemaphoreType.DMA((4,)),
        ]
        + round_scratch(),
        compiler_params=pltpu.CompilerParams(collective_id=0, has_side_effects=True, vmem_limit_bytes=VMEM_LIMIT),
        name="gather",
    )(features, coarse_grad.reshape(1024, 216), *lists, jnp.asarray(select_in(True)), swap)
    fine, contrib, pre, grads = pl.pallas_call(
        compute_kernel,
        out_shape=(
            struct((B, C, VOX), BF),
            struct((B, C2, 216), BF),
            struct((B, ROWS, 256), BF),
            struct((GROWS, 128), F32),
        ),
        in_specs=[VM] * 11,
        out_specs=(VM,) * 4,
        scratch_shapes=[
            pltpu.VMEM((B * ROWS, TAPS * 256), BF),
            pltpu.VMEM((256, TAPS * 256), BF),
            pltpu.VMEM((512, 256), BF),
            pltpu.VMEM((B, ROWS, 256), F32),
            pltpu.VMEM((768, 256), BF),
            pltpu.VMEM((B, 256, ROWS), BF),
            pltpu.VMEM((B, 256, ROWS), BF),
            pltpu.VMEM((B * ROWS, 256), BF),
        ],
        compiler_params=pltpu.CompilerParams(vmem_limit_bytes=VMEM_LIMIT),
        name="compute",
    )(
        pad, fine_grad, child, conv_weight, down_weight,
        jnp.asarray(select_in(False)), sel_out, jnp.asarray(sel_down), jnp.asarray(sel_up), jnp.asarray(sel_spread), eye,
    )
    padded_grad, coarse_out, grad_conv, grad_down = pl.pallas_call(
        reduce_kernel,
        out_shape=(
            struct((B, 2, PROWS, 128), F32),
            struct((1024, 216), BF),
            struct((27, C, C), F32),
            struct((8, C2, C), F32),
        ),
        in_specs=[VM] * 3 + [SM] * 5 + [VM],
        out_specs=(VM,) * 4,
        scratch_shapes=[
            pltpu.VMEM((B, 2, PROWS, 128), F32),
            pltpu.VMEM((4, C2, 216), BF),
            pltpu.VMEM((5, C2, 216), BF),
            pltpu.SemaphoreType.DMA((4,)),
            pltpu.SemaphoreType.DMA((4,)),
            pltpu.VMEM((N_OWNER, CHUNK, 128), F32),
            pltpu.VMEM((N_REGION, CHUNK, 128), F32),
            pltpu.VMEM((N_OWNER, CHUNK, 128), F32),
            pltpu.SemaphoreType.DMA((N_OWNER,)),
            pltpu.SemaphoreType.DMA((N_OWNER,)),
            pltpu.SemaphoreType.DMA((N_REGION,)),
            pltpu.SemaphoreType.DMA((N_REGION,)),
            pltpu.SemaphoreType.DMA((N_OWNER,)),
            pltpu.SemaphoreType.DMA((N_OWNER,)),
        ]
        + round_scratch(),
        compiler_params=pltpu.CompilerParams(collective_id=1, has_side_effects=True, vmem_limit_bytes=VMEM_LIMIT),
        name="reduce",
    )(pre, contrib, grads.reshape(N_OWNER, CHUNK, 128), *lists, swap)
    grad_in = pl.pallas_call(
        back_kernel,
        out_shape=struct((B, C, VOX), BF),
        in_specs=[VM] * 4,
        out_specs=VM,
        scratch_shapes=[
            pltpu.VMEM((ROWS, TAPS * 256), BF),
            pltpu.VMEM((TAPS * 256, 256), BF),
            pltpu.VMEM((768, 256), BF),
        ],
        compiler_params=pltpu.CompilerParams(vmem_limit_bytes=VMEM_LIMIT),
        name="back",
    )(padded_grad, conv_weight, sel_out, eye)
    return fine, coarse_out.reshape(1, C2, 8, 216), grad_in, grad_conv, grad_down


def solution(mesh):
    both = ("region", "owner")
    return jax.shard_map(
        local,
        mesh=mesh,
        in_specs=(
            P(both, None, None),
            P(),
            P(),
            P(both, None, None),
            P(both, None, None, None),
            P(both, None, None, None),
            P(both, None, None),
            P(both, None),
            P(both, None),
            P(both, None),
        ),
        out_specs=(P(both, None, None), P(both, None, None, None), P(both, None, None), P(), P()),
        check_vma=False,
    )
```

profile of v0, /device:TPU:1, one launch (start us, length us, event | category | flops | bytes accessed | tf_op | source)
XLA Modules:
  0.0 145.9 jit_solution(509965238474594108)
XLA Ops:
  0.6 1.3 copy.26.z_list
  1.9 1.4 copy.24.send_list
  3.3 1.4 copy.25.recv_list
  4.6 1.7 %copy.27.down = bf16[8,128,64]{2,1,0:T(8,128)(2,1)} copy(bf16[8,128,64]{1,2,0:T(8,128)(2,1)} %param.20) | data formatting | bytes 262144 | tf_op args[2]
  6.4 2.2 %copy.23 = bf16[1,128,8,216]{3,2,1,0:T(8,128)(2,1)} copy(bf16[1,128,8,216]{1,3,2,0:T(8,128)(2,1)} %param.22) | data formatting | bytes 884736 | tf_op args[4]
  8.6 30.6 %gather.1 = (f32[4,2,784,128]{3,2,1,0:T(8,128)}, bf16[4,128,216]{2,1,0:T(8,128)(2,1)}) custom-call(bf16[4,64,1728]{2,1,0:T(8,128)(2,1)} %feat.1, bf16[1024,216]{1,0:T(8,128)(2,1)} %bitcast.3, s32[1,2,4,2]{3,2,1,0:T(4,128)} %copy.24.send_list, s32[4,2,2]{2,1,0:T(2,128)} %copy.25.recv_list, s32[4,2]{1,0:T(4,128)} %copy.26.z_list, s32[1,4]{1,0:T(1,128)} %p_send.3, ...), custom_call_target="tpu_custom_call" | custom-call | tf_op jit(solution)/shard_map/gather/pallas_call | solution.py:642
  39.1 26.9 %compute.1 = (bf16[4,64,1728]{2,1,0:T(8,128)(2,1)}, bf16[4,128,216]{2,1,0:T(8,128)(2,1)}, bf16[4,576,256]{2,1,0:T(8,128)(2,1)}, f32[1536,128]{1,0:T(8,128)}) custom-call(f32[4,2,784,128]{3,2,1,0:T(8,128)} %get-tuple-element.15.pad, bf16[4,64,1728]{2,1,0:T(8,128)(2,1)} %fgrad.1, bf16[4,128,216]{2,1,0:T(8,128)(2,1)} %get-tuple-element.16.child, ...), custom_call_target="tpu_custom_call" | custom-call | tf_op jit(solution)/shard_map/compute/pallas_call | solution.py:658
  66.0 61.0 %reduce.1 = (f32[4,2,784,128]{3,2,1,0:T(8,128)}, bf16[1024,216]{1,0:T(8,128)(2,1)}, f32[27,64,64]{2,1,0:T(8,128)}, f32[8,128,64]{2,1,0:T(8,128)}) custom-call(bf16[4,576,256]{2,1,0:T(8,128)(2,1)} %get-tuple-element.18.pre, bf16[4,128,216]{2,1,0:T(8,128)(2,1)} %get-tuple-element.19.contrib, f32[32,48,128]{2,1,0:T(8,128)} %bitcast.4, ...), custom_call_target="tpu_custom_call" | custom-call | tf_op jit(solution)/shard_map/reduce/pallas_call | solution.py:684
  127.0 0.0 copy-start
  127.0 2.3 %copy.31 = bf16[1,128,8,216]{1,3,2,0:T(8,128)(2,1)} copy(bf16[1,128,8,216]{3,2,1,0:T(8,128)(2,1)} %bitcast.5) | data formatting | bytes 884736
  129.3 1.9 %copy.32 = f32[8,128,64]{1,2,0:T(8,128)} copy(f32[8,128,64]{2,1,0:T(8,128)} %get-tuple-element.29) | data formatting | bytes 524288
  131.2 13.7 %back.1 = bf16[4,64,1728]{2,1,0:T(8,128)(2,1)} custom-call(f32[4,2,784,128]{3,2,1,0:T(8,128)} %get-tuple-element.22.pad, bf16[27,64,64]{2,1,0:T(8,128)(2,1)} %weight.3, bf16[2,256,288]{2,1,0:T(8,128)(2,1)} %constant.18.clone.sel_out, bf16[256,256]{1,0:T(8,128)(2,1)} %constant.17.clone.eye), custom_call_target="tpu_custom_call" | custom-call | tf_op jit(solution)/shard_map/back/pallas_call | solution.py:714
  144.9 0.0 copy-done
  144.9 0.9 copy.34
Async XLA Ops:
  127.0 17.9 %copy-start = (f32[27,64,64]{2,1,0:T(8,128)S(1)}, f32[27,64,64]{2,1,0:T(8,128)}, u32[]{:S(2)}) copy-start(f32[27,64,64]{2,1,0:T(8,128)} %get-tuple-element.38) | copy-start | bytes 1327108
where the time goes:
time: 147 us; the launch traced here: 146 us
  Pallas kernels  132 us (90%)
  local copies, waits for them, and re-layouts  13.1 us (9%)
    pallas_call x1, Pallas kernels, local(): pl.pallas_call(reduce_kernel, out_shape=(struct((B, 2, PROWS, 128), F32),...  61 us
    pallas_call x1, Pallas kernels, local(): pl.pallas_call(gather_kernel, out_shape=(struct((B, 2, PROWS, 128), F32),...  30.6 us
    pallas_call x1, Pallas kernels, local(): pl.pallas_call(compute_kernel, out_shape=(struct((B, C, VOX), BF), struct...  26.9 us
    pallas_call x1, Pallas kernels, local(): pl.pallas_call(back_kernel, out_shape=struct((B, C, VOX), BF), in_specs=[...  13.7 us
    unnamed x10, local copies, waits for them, and re-layouts  13.1 us

commit v1 on v0

v1 whole, which is shorter than its diff:
```python
import math

import jax
import jax.numpy as jnp
import numpy as np
from jax import lax
from jax.experimental import pallas as pl
from jax.experimental.pallas import tpu as pltpu
from jax.sharding import PartitionSpec as P


C = 64
C2 = 128
VOX = 1728
B = 4
PROWS = 14 * 7 * 8
ROWS = 6 * 6 * 16
TAPS = 12
OFFSETS = (1, -1, 2, -2)
N_OWNER = 32
N_REGION = 8
CHUNK = 48
GROWS = N_OWNER * CHUNK
BF = jnp.bfloat16
F32 = jnp.float32
MESH = pl.DeviceIdType.MESH
VMEM_LIMIT = 56 * 1024 * 1024


def select_in(padded):
    count = 7 if padded else 6
    back = 1 if padded else 0
    out = np.zeros((8, 4, count * 8, 256), np.float32)
    for v in range(8):
        for e in range(2):
            for f in range(2):
                for jj in range(count):
                    for ll in range(count):
                        j, l = 2 * jj + e - back, 2 * ll + f - back
                        if 0 <= j < 12 and 0 <= l < 12:
                            col = 16 * v + j * 12 + l
                            if col < 256:
                                out[v, 2 * e + f, jj * 8 + ll, col] = 1
    return out.reshape(8, 4 * count * 8, 256).astype(BF)


def select_out():
    out = np.zeros((2, 2, 128, 288), np.float32)
    for e in range(2):
        for f in range(2):
            for jj in range(6):
                for s in range(2):
                    for ll in range(6):
                        out[e, f, jj * 16 + s * 8 + ll, s * 144 + (2 * jj + e) * 12 + 2 * ll + f] = 1
    return out.reshape(2, 256, 288).astype(BF)


def coarse_selects():
    up = np.zeros((288, 216), np.float32)
    for ii in range(6):
        for jj in range(6):
            for ll in range(6):
                up[(ii * 6 + jj) * 8 + ll, ii * 36 + jj * 6 + ll] = 1
    return up.astype(BF), up.T.copy().astype(BF)


def dot(a, b):
    return jnp.dot(a, b, preferred_element_type=F32)


def dot_t(a, b):
    return lax.dot_general(a, b, (((1,), (1,)), ((), ())), preferred_element_type=F32)


def low_lanes(rows):
    return lax.broadcasted_iota(jnp.int32, (rows, 128), 1) < 64


def to_rows(src_ref, sel_ref, count, put):
    nr = count * 8
    low = low_lanes(nr)
    for i in range(12):
        start = (144 * i) // 128 * 128
        width = min(256, VOX - start)
        window = src_ref[:, :, start : start + width].reshape(B * C, width)
        rows = dot_t(sel_ref[i % 8, :, :width], window)
        for e in range(2):
            for pair in range(2):
                lanes = slice(pair * 128, pair * 128 + 128)
                first = rows[2 * e * nr : (2 * e + 1) * nr, lanes]
                second = rows[(2 * e + 1) * nr : (2 * e + 2) * nr, lanes]
                put(2 * pair, i, e, jnp.where(low, first, pltpu.roll(second, 64, 1)))
                put(2 * pair + 1, i, e, jnp.where(low, pltpu.roll(first, 64, 1), second))


def from_rows(turned, sel_ref):
    total = None
    for e in range(2):
        blocks = [
            jnp.concatenate(
                [turned[(2 * e + f) * 64 : (2 * e + f + 1) * 64, ii * 128 : ii * 128 + 128] for f in range(2)], axis=1
            )
            for ii in range(6)
        ]
        part = dot(jnp.concatenate(blocks, axis=0), sel_ref[e])
        total = part if total is None else total + part
    return jnp.concatenate([total[ii * 64 : ii * 64 + 64] for ii in range(6)], axis=1)


def im2col(pad_ref, b, put):
    def step(ii, carry):
        for e in range(2):
            slabs = pad_ref[b, e, pl.ds(pl.multiple_of(ii * 112, 8), 224), :]
            shifted = pltpu.roll(slabs, 223, 0)
            for a in range(3):
                for dj in range(2):
                    for dl, source in ((0, slabs), (1, shifted)):
                        pieces = []
                        for jj in range(6):
                            for s in range(2):
                                row = ((a + s) * 7 + jj + dj) * 8
                                pieces.append(source[row : row + 8])
                        put(ii, ((a * 2 + dj) * 2 + dl) * 2 + e, jnp.concatenate(pieces, axis=0).astype(BF))
        return carry

    lax.fori_loop(0, 6, step, 0)


class Rounds:
    def __init__(self, pad, send_list, recv_list, z_list, bufs):
        self.pad, self.send_list, self.recv_list, self.z_list = pad, send_list, recv_list, z_list
        (self.sx, self.rx, self.sy, self.ry, self.sz, self.rz, self.ssem, self.rsem) = bufs
        self.region = lax.axis_index("region")
        self.owner = lax.axis_index("owner")

    def owner_copies(self, send, recv, base):
        out = []
        for m, t in enumerate(OFFSETS):
            out.append(
                pltpu.make_async_remote_copy(
                    src_ref=send.at[pl.ds(2 * m, 2)],
                    dst_ref=recv.at[pl.ds(2 * m, 2)],
                    send_sem=self.ssem.at[base + m],
                    recv_sem=self.rsem.at[base + m],
                    device_id=(self.region, lax.rem(self.owner + (t + N_OWNER), N_OWNER)),
                    device_id_type=MESH,
                )
            )
        return out

    def x_copies(self):
        return self.owner_copies(self.sx, self.rx, 0)

    def y_copies(self):
        return self.owner_copies(self.sy, self.ry, 4)

    def z_copies(self):
        out = []
        for m, t in enumerate((1, N_REGION - 1)):
            out.append(
                pltpu.make_async_remote_copy(
                    src_ref=self.sz.at[pl.ds(4 * m, 4)],
                    dst_ref=self.rz.at[pl.ds(4 * m, 4)],
                    send_sem=self.ssem.at[8 + m],
                    recv_sem=self.rsem.at[8 + m],
                    device_id=(lax.rem(self.region + t, N_REGION), self.owner),
                    device_id_type=MESH,
                )
            )
        return out

    def x_start(self):
        for n in range(8):
            pick = self.send_list[0, 0, n % 2, n // 2]
            slot, high = lax.rem(pick, 4), pick >= 4
            for e in range(2):
                low_face = self.pad[slot, e, 56:112, :]
                high_face = self.pad[slot, e, 672:728, :]
                self.sx[n, :, e * 128 : e * 128 + 128] = jnp.where(high, high_face, low_face).astype(BF)
        for copy in self.x_copies():
            copy.start()

    def x_end(self):
        for copy in self.x_copies():
            copy.wait_recv()
        for b in range(B):
            low_pad = self.rx[jnp.maximum(self.recv_list[0, 0, b] - 8, 0)].astype(F32)
            high_pad = self.rx[jnp.maximum(self.recv_list[0, 1, b] - 8, 0)].astype(F32)
            for e in range(2):
                self.pad[b, e, 0:56, :] = low_pad[:, e * 128 : e * 128 + 128]
                self.pad[b, e, 728:784, :] = high_pad[:, e * 128 : e * 128 + 128]

    def y_start(self):
        for n in range(8):
            pick = self.send_list[0, 1, n % 2, n // 2]
            slot, high = lax.rem(pick, 4), pick >= 4
            faces = []
            for i in range(14):
                low_face = self.pad[slot, 1, i * 56 : i * 56 + 8, :]
                high_face = self.pad[slot, 0, i * 56 + 48 : i * 56 + 56, :]
                faces.append(jnp.where(high, high_face, low_face))
            self.sy[n] = jnp.concatenate(faces, axis=0).astype(BF)
        for copy in self.y_copies():
            copy.start()

    def y_end(self):
        for copy in self.y_copies():
            copy.wait_recv()
        for b in range(B):
            low_pad = self.ry[jnp.maximum(self.recv_list[1, 0, b] - 8, 0)].astype(F32)
            high_pad = self.ry[jnp.maximum(self.recv_list[1, 1, b] - 8, 0)].astype(F32)
            for i in range(14):
                self.pad[b, 0, i * 56 : i * 56 + 8, :] = low_pad[i * 8 : i * 8 + 8]
                self.pad[b, 1, i * 56 + 48 : i * 56 + 56, :] = high_pad[i * 8 : i * 8 + 8]

    def z_start(self):
        low = low_lanes(98)
        for b in range(B):
            tiles = [self.pad[b, e, pl.ds(6, 98, stride=8), :] for e in range(2)]
            self.sz[b] = jnp.where(low, tiles[0], pltpu.roll(tiles[1], 64, 1)).astype(BF)
            tiles = [self.pad[b, e, pl.ds(0, 98, stride=8), :] for e in range(2)]
            self.sz[4 + b] = jnp.where(low, pltpu.roll(tiles[0], 64, 1), tiles[1]).astype(BF)
        for copy in self.z_copies():
            copy.start()

    def z_end(self):
        for copy in self.z_copies():
            copy.wait_recv()
        low = low_lanes(98)
        for b in range(B):
            for side in range(2):
                pick = self.z_list[side, b]
                zero = (pick == 8) | ((pick < 4) & (self.region == 0)) | ((pick >= 4) & (self.region == N_REGION - 1))
                face = self.rz[jnp.minimum(pick, 7)].astype(F32)
                face = jnp.where(zero, jnp.zeros_like(face), face)
                turned = pltpu.roll(face, 64, 1)
                row = 6 * side
                for e in range(2):
                    at = (b, e, pl.ds(row, 98, stride=8))
                    tile = self.pad[at]
                    if side == 0:
                        self.pad[at] = jnp.where(low, turned if e else face, tile)
                    else:
                        self.pad[at] = jnp.where(low, tile, face if e else turned)

    def drain(self):
        for copy in self.x_copies() + self.y_copies() + self.z_copies():
            copy.wait_send()


def round_scratch():
    return [
        pltpu.VMEM((8, 56, 256), BF),
        pltpu.VMEM((8, 56, 256), BF),
        pltpu.VMEM((8, 112, 128), BF),
        pltpu.VMEM((8, 112, 128), BF),
        pltpu.VMEM((8, 98, 128), BF),
        pltpu.VMEM((8, 98, 128), BF),
        pltpu.SemaphoreType.DMA((10,)),
        pltpu.SemaphoreType.DMA((10,)),
    ]


class Barrier:
    def __init__(self):
        self.region, self.owner = lax.axis_index("region"), lax.axis_index("owner")
        self.barrier = pltpu.get_barrier_semaphore()

    def signal(self):
        def one_owner(d, carry):
            to = (self.region, lax.rem(self.owner + d, N_OWNER))
            pl.semaphore_signal(self.barrier, inc=1, device_id=to, device_id_type=MESH)
            return carry

        def one_region(d, carry):
            to = (lax.rem(self.region + d, N_REGION), self.owner)
            pl.semaphore_signal(self.barrier, inc=1, device_id=to, device_id_type=MESH)
            return carry

        lax.fori_loop(1, N_OWNER, one_owner, 0)
        lax.fori_loop(1, N_REGION, one_region, 0)

    def wait(self):
        pl.semaphore_wait(self.barrier, N_OWNER + N_REGION - 2)


def forward_weights(weight, wide):
    zero = jnp.zeros((64, 64), BF)
    for e1 in range(2):
        for f1 in range(2):
            for k in range(TAPS):
                a, dj, dl = k // 4, k // 2 % 2, k % 2
                for e in range(2):
                    te = 2 * dj + e - e1
                    blocks = []
                    for f in range(2):
                        tf = 2 * dl + f - f1
                        ok = 0 <= te < 3 and 0 <= tf < 3
                        blocks.append(weight[9 * a + 3 * te + tf] if ok else zero)
                    row, lane = (2 * e1 + f1) * 64, k * 256 + e * 128
                    wide[row : row + 64, lane : lane + 128] = jnp.concatenate(blocks, axis=1)


def backward_weights(weight, tall):
    zero = jnp.zeros((64, 64), BF)
    for e1 in range(2):
        for k in range(TAPS):
            a, dj, dl = k // 4, k // 2 % 2, k % 2
            for e in range(2):
                te = 2 * dj + e - e1
                for f in range(2):
                    blocks = []
                    for f1 in range(2):
                        tf = 2 * dl + f - f1
                        ok = 0 <= te < 3 and 0 <= tf < 3
                        blocks.append(weight[9 * (2 - a) + 3 * (2 - te) + 2 - tf] if ok else zero)
                    row = k * 256 + (2 * e + f) * 64
                    tall[row : row + 64, e1 * 128 : e1 * 128 + 128] = jnp.concatenate(blocks, axis=1)


def pad_rows(pad, b, rows):
    low = low_lanes(48)
    edge = jnp.zeros((8, 128), F32)
    for e in range(2):
        pad[b, e, 0:56, :] = jnp.zeros((56, 128), F32)
        pad[b, e, 728:784, :] = jnp.zeros((56, 128), F32)
    for ii in range(6):
        for s in range(2):
            to = (2 * ii + s + 1) * 56
            for e in range(2):
                tile = jnp.concatenate(
                    [
                        rows[ii * 96 + jj * 16 + s * 8 : ii * 96 + jj * 16 + s * 8 + 8, e * 128 : e * 128 + 128]
                        for jj in range(6)
                    ],
                    axis=0,
                )
                tile = pltpu.roll(tile, 64, 1)
                tile = jnp.where(low, pltpu.roll(tile, 1, 0), tile)
                if e == 0:
                    pad[b, 1, to : to + 48, :] = tile
                    pad[b, 1, to + 48 : to + 56, :] = edge
                else:
                    pad[b, 0, to + 8 : to + 56, :] = tile
                    pad[b, 0, to : to + 8, :] = edge


def fold_conv(turned, cols, grads):
    low = low_lanes(64)
    main = [[None] * 3 for _ in range(3)]
    last = [[None] * 3 for _ in range(3)]

    def add(total, value):
        return value if total is None else total + value

    for a in range(3):
        for dj in range(2):
            tiles = []
            for dl in range(2):
                k = (a * 2 + dj) * 2 + dl
                total = None
                for b in range(B):
                    total = add(total, dot(turned[b], cols[b * ROWS : (b + 1) * ROWS, k * 256 : k * 256 + 256]))
                tiles.append(total)
            for e1 in range(2):
                for e in range(2):
                    te = 2 * dj + e - e1
                    if not 0 <= te < 3:
                        continue
                    lanes = slice(e * 128, e * 128 + 128)
                    t0, t1 = (tiles[dl][e1 * 128 : e1 * 128 + 64, lanes] for dl in range(2))
                    main[a][te] = add(main[a][te], t0)
                    last[a][te] = add(last[a][te], t1)
                    t0, t1 = (pltpu.roll(tiles[dl][e1 * 128 + 64 : e1 * 128 + 128, lanes], 64, 1) for dl in range(2))
                    main[a][te] = add(main[a][te], jnp.where(low, t0, t1))
                    last[a][te] = add(last[a][te], t1)
    main = main[0] + main[1] + main[2]
    last = last[0] + last[1] + last[2]

    def put(row, value):
        for start, size, part, at in split_rows(row, 64):
            grads[part, at : at + size, :] = value[start : start + size]

    for n in range(9):
        put(n * 64, main[n])
    for n in range(5):
        other = pltpu.roll(last[2 * n + 1], 64, 1) if n < 4 else jnp.zeros((64, 128), F32)
        put(576 + n * 64, jnp.where(low, last[2 * n], other))


def split_rows(row, count):
    out, start = [], 0
    while start < count:
        part, at = divmod(row + start, CHUNK)
        size = min(count - start, CHUNK - at)
        out.append((start, size, part, at))
        start += size
    return out


def step_kernel(
    feat, weight, down, fgrad, coarse_in, send_list, recv_list, z_list, p_send, p_recv,
    sel_in, sel_fg, sel_out, sel_up, sel_down, eye,
    fine, coarse, grad_in, conv_out, down_out,
    pad, cols, wide, tall, mats, fg, rows8, turned, grad_turned, kids, child, grads,
    csend, crecv, dsend, drecv, first, second, mine, third, cs, cr, ds, dr, s1, r1, s2, r2, s3, r3, *bufs,
):
    region, owner = lax.axis_index("region"), lax.axis_index("owner")
    barrier = Barrier()
    barrier.signal()
    half = len(bufs) // 2
    ahead = Rounds(pad, send_list, recv_list, z_list, bufs[:half])
    back = Rounds(pad, send_list, recv_list, z_list, bufs[half:])

    def to_owner(src, dst, send, recv, shift):
        return pltpu.make_async_remote_copy(
            src_ref=src, dst_ref=dst, send_sem=send, recv_sem=recv,
            device_id=(region, lax.rem(owner + shift, N_OWNER)), device_id_type=MESH,
        )

    def leg1(d):
        return to_owner(grads.at[lax.rem(owner + d, N_OWNER)], first.at[d], s1.at[d], r1.at[d], d)

    def leg2(d):
        return pltpu.make_async_remote_copy(
            src_ref=second.at[region], dst_ref=second.at[region], send_sem=s2.at[d], recv_sem=r2.at[d],
            device_id=(lax.rem(region + d, N_REGION), owner), device_id_type=MESH,
        )

    def leg3(d):
        return to_owner(mine, third.at[owner], s3.at[d], r3.at[d], d)

    def each(count, leg, what):
        def body(d, carry):
            getattr(leg(d), what)()
            return carry

        lax.fori_loop(1, count, body, 0)

    def put(b, i, e, value):
        pad[b, e, (i + 1) * 56 : (i + 2) * 56, :] = value

    to_rows(feat, sel_in, 7, put)
    barrier.wait()
    ahead.x_start()
    kid_copies = [to_owner(csend.at[m], crecv.at[m], cs.at[m], cr.at[m], N_OWNER - m - 1) for m in range(4)]
    for m in range(4):
        index = jnp.int32(0)
        for q in range(8):
            index = jnp.where(p_recv[0, q] == m, q, index)
        csend[m] = coarse_in[index]
        kid_copies[m].start()
    forward_weights(weight, wide)
    ahead.x_end()
    ahead.y_start()

    def put_grad(b, i, e, value):
        for jj in range(6):
            row = ((i // 2) * 6 + jj) * 16 + (i % 2) * 8
            fg[b, row : row + 8, e * 128 : e * 128 + 128] = value[jj * 8 : jj * 8 + 8]

    to_rows(fgrad, sel_fg, 6, put_grad)
    ahead.y_end()
    ahead.z_start()
    for s in range(2):
        mats[s] = jnp.concatenate([down[4 * s + n] for n in range(4)], axis=0)
    for b in range(B):
        for ii in range(6):
            rows8[b, ii * 128 + 96 : ii * 128 + 128, :] = jnp.zeros((32, 256), BF)
    for copy in kid_copies:
        copy.wait_recv()
    for k in range(B):
        index = jnp.int32(0)
        for m in range(4):
            index = jnp.where(p_send[0, m] == k, m, index)
        child[k] = crecv[index]
    backward_weights(weight, tall)
    ahead.z_end()

    live = lax.rem(lax.broadcasted_iota(jnp.int32, (ROWS, 256), 0), 8) < 6
    blank = jnp.zeros((8, 128), F32)

    def brick(b, carry):
        base = pl.multiple_of(b * ROWS, 16)

        def put(ii, k, value):
            cols[pl.ds(pl.multiple_of(base + ii * 96, 16), 96), k * 128 : k * 128 + 128] = value

        im2col(pad, b, put)
        act = dot_t(cols[pl.ds(base, ROWS), :], wide[...])
        sig = 1.0 / (1.0 + jnp.exp(-act))
        rows = (act * sig).astype(BF)
        for ii in range(6):
            rows8[b, ii * 128 : ii * 128 + 96, :] = rows[ii * 96 : ii * 96 + 96]
        slope = sig * (1.0 + act * (1.0 - sig))
        up = dot(sel_up[...], child[b])
        halves = [dot_t(up.astype(BF), mats[s]) for s in range(2)]
        pieces, kid = [], []
        for t in range(36):
            cut = up[t * 8 : t * 8 + 8]
            kid += [jnp.concatenate([cut, blank], axis=1), jnp.concatenate([blank, cut], axis=1)]
            for s in range(2):
                pieces.append(halves[s][t * 8 : t * 8 + 8])
        kids[pl.ds(base, ROWS), :] = jnp.concatenate(kid, axis=0).astype(BF)
        grad = (fg[b] + jnp.concatenate(pieces, axis=0)) * slope
        grad = jnp.where(live, grad, 0.0).astype(BF)
        grad_turned[b] = dot_t(eye[...], grad).astype(BF)
        pad_rows(pad, b, grad.astype(F32))
        return carry

    lax.fori_loop(0, B, brick, 0)
    back.x_start()

    def contribution(b, carry):
        pieces = [
            dot(jnp.concatenate([rows8[b, ii * 128 : ii * 128 + 96, :] for ii in range(6)], axis=0), mats[s])
            for s in range(2)
        ]
        sums = [pieces[0][t * 16 : t * 16 + 8] + pieces[1][t * 16 + 8 : t * 16 + 16] for t in range(36)]
        coarse_tmp = dot(sel_down[...], jnp.concatenate(sums, axis=0).astype(BF)).astype(BF)
        child[b] = coarse_tmp
        turned[b] = dot_t(eye[...], rows8[b]).astype(BF)
        return carry

    lax.fori_loop(0, B, contribution, 0)
    up_copies = [to_owner(dsend.at[m], drecv.at[m], ds.at[m], dr.at[m], m + 1) for m in range(4)]
    for m in range(4):
        dsend[m] = child[p_send[0, m]]
        up_copies[m].start()

    fold_conv(grad_turned, cols, grads)
    total = None
    for b in range(B):
        short = jnp.concatenate([turned[b, :, ii * 128 : ii * 128 + 96] for ii in range(6)], axis=1)
        part = dot(short, kids[b * ROWS : (b + 1) * ROWS, :])
        total = part if total is None else total + part
    for s in range(2):
        for start, size, part, at in split_rows(896 + s * 256, 256):
            grads[part, at : at + size, :] = total[start : start + size, s * 128 : s * 128 + 128]
    for start, size, part, at in split_rows(1408, 128):
        grads[part, at : at + size, :] = jnp.zeros((size, 128), F32)
    each(N_OWNER, leg1, "start")
    back.x_end()
    back.y_start()
    for b in range(2):
        fine[b] = from_rows(turned[b], sel_out).astype(BF)
    back.y_end()
    back.z_start()
    for b in range(2, B):
        fine[b] = from_rows(turned[b], sel_out).astype(BF)
    for copy in up_copies:
        copy.wait_recv()
    drecv[4] = jnp.zeros((216, C2), BF)
    for q in range(8):
        coarse[q] = drecv[p_recv[0, q]]
    back.z_end()

    def back_brick(b, carry):
        def put(ii, k, value):
            cols[pl.ds(pl.multiple_of(ii * 96, 16), 96), k * 128 : k * 128 + 128] = value

        im2col(pad, b, put)
        rows = dot(cols[pl.ds(0, ROWS), :], tall[...]).astype(BF)
        for ii in range(6):
            rows8[b, ii * 128 : ii * 128 + 96, :] = rows[ii * 96 : ii * 96 + 96]
        grad_in[b] = from_rows(dot_t(eye[...], rows8[b]).astype(BF), sel_out).astype(BF)
        return carry

    lax.fori_loop(0, 1, back_brick, 0)
    each(N_OWNER, leg1, "wait_recv")
    second[region] = lax.fori_loop(1, N_OWNER, lambda d, total: total + first[d], grads[owner])
    each(N_REGION, leg2, "start")
    lax.fori_loop(1, 3, back_brick, 0)
    each(N_REGION, leg2, "wait_recv")
    part = lax.fori_loop(1, N_REGION, lambda d, total: total + second[d], second[0])
    factor = 1.0 / math.sqrt(B * N_OWNER * N_REGION * VOX)
    part = (part * factor).astype(BF)
    mine[...] = part
    each(N_OWNER, leg3, "start")
    third[owner] = part
    lax.fori_loop(3, B, back_brick, 0)
    each(N_OWNER, leg3, "wait_recv")
    total = third[...].astype(F32).reshape(GROWS, 128)
    for n in range(9):
        tile = total[n * 64 : n * 64 + 64]
        conv_out[3 * n] = tile[:, 0:64]
        conv_out[3 * n + 1] = tile[:, 64:128]
        row = 576 + (n // 2) * 64
        conv_out[3 * n + 2] = total[row : row + 64, (n % 2) * 64 : (n % 2) * 64 + 64]
    for t in range(8):
        down_out[t] = total[896 + t * 64 : 960 + t * 64]
    ahead.drain()
    back.drain()
    for copy in kid_copies + up_copies:
        copy.wait_send()
    each(N_OWNER, leg1, "wait_send")
    each(N_REGION, leg2, "wait_send")
    each(N_OWNER, leg3, "wait_send")


VM = pl.BlockSpec(memory_space=pltpu.VMEM)
SM = pl.BlockSpec(memory_space=pltpu.SMEM)


def struct(shape, kind):
    return jax.ShapeDtypeStruct(shape, kind)


def local(
    features, conv_weight, down_weight, fine_grad, coarse_grad, face_send, face_recv, z_recv, parent_send, parent_recv
):
    sel_up, sel_down = coarse_selects()
    consts = (select_in(True), select_in(False), select_out(), sel_up, sel_down, np.eye(256, dtype=np.float32).astype(BF))
    dma = pltpu.SemaphoreType.DMA
    fine, coarse_out, grad_in, grad_conv, grad_down = pl.pallas_call(
        step_kernel,
        out_shape=(
            struct((B, C, VOX), BF),
            struct((8, 216, C2), BF),
            struct((B, C, VOX), BF),
            struct((27, C, C), F32),
            struct((8, C, C2), F32),
        ),
        in_specs=[VM] * 5 + [SM] * 5 + [VM] * 6,
        out_specs=(VM,) * 5,
        scratch_shapes=[
            pltpu.VMEM((B, 2, PROWS, 128), F32),
            pltpu.VMEM((B * ROWS, TAPS * 256), BF),
            pltpu.VMEM((256, TAPS * 256), BF),
            pltpu.VMEM((TAPS * 256, 256), BF),
            pltpu.VMEM((2, 256, C2), BF),
            pltpu.VMEM((B, ROWS, 256), F32),
            pltpu.VMEM((B, 768, 256), BF),
            pltpu.VMEM((B, 256, 768), BF),
            pltpu.VMEM((B, 256, ROWS), BF),
            pltpu.VMEM((B * ROWS, 256), BF),
            pltpu.VMEM((B, 216, C2), BF),
            pltpu.VMEM((N_OWNER, CHUNK, 128), F32),
            pltpu.VMEM((4, 216, C2), BF),
            pltpu.VMEM((4, 216, C2), BF),
            pltpu.VMEM((4, 216, C2), BF),
            pltpu.VMEM((5, 216, C2), BF),
            pltpu.VMEM((N_OWNER, CHUNK, 128), F32),
            pltpu.VMEM((N_REGION, CHUNK, 128), F32),
            pltpu.VMEM((CHUNK, 128), BF),
            pltpu.VMEM((N_OWNER, CHUNK, 128), BF),
        ]
        + [dma((4,))] * 4
        + [dma((N_OWNER,))] * 2
        + [dma((N_REGION,))] * 2
        + [dma((N_OWNER,))] * 2
        + round_scratch()
        + round_scratch(),
        compiler_params=pltpu.CompilerParams(collective_id=0, has_side_effects=True, vmem_limit_bytes=VMEM_LIMIT),
        name="step",
    )(
        features, conv_weight, down_weight.transpose(0, 2, 1), fine_grad, coarse_grad[0].transpose(1, 2, 0),
        face_send.transpose(0, 1, 3, 2), face_recv.transpose(1, 2, 0), z_recv.transpose(1, 0), parent_send, parent_recv,
        *(jnp.asarray(c) for c in consts),
    )
    return fine, coarse_out.transpose(2, 0, 1)[None], grad_in, grad_conv, grad_down.transpose(0, 2, 1)


def solution(mesh):
    both = ("region", "owner")
    return jax.shard_map(
        local,
        mesh=mesh,
        in_specs=(
            P(both, None, None),
            P(),
            P(),
            P(both, None, None),
            P(both, None, None, None),
            P(both, None, None, None),
            P(both, None, None),
            P(both, None),
            P(both, None),
            P(both, None),
        ),
        out_specs=(P(both, None, None), P(both, None, None, None), P(both, None, None), P(), P()),
        check_vma=False,
    )
```

time: 147 us -> 91.4 us (0.62)
  Pallas kernels: 132 us -> 84.2 us
  local copies, waits for them, and re-layouts: 13.1 us -> 6.33 us
    pallas_call x4 -> x1, Pallas kernels: 132 us -> 84.2 us  [local(): pl.pallas_call(step_kernel, out_shape=(struct((B, C, VOX), BF), struct((8...]
    unnamed x10 -> x13, local copies, waits for them, and re-layouts: 13.1 us -> 6.33 us
where the time goes in v1:
time: 91.4 us; the launch traced here: 91.2 us
  Pallas kernels  84.2 us (92%)
  local copies, waits for them, and re-layouts  6.33 us (7%)
    pallas_call x1, Pallas kernels, local(): pl.pallas_call(step_kernel, out_shape=(struct((B, C, VOX), BF), struct((8...  84.2 us
    unnamed x13, local copies, waits for them, and re-layouts  6.33 us

profile of v1, /device:TPU:1, one launch (start us, length us, event | category | flops | bytes accessed | tf_op | source)
XLA Modules:
  0.0 91.2 jit_solution(11443096435182511342)
XLA Ops:
  0.6 84.2 %step.1 = (bf16[4,64,1728]{2,1,0:T(8,128)(2,1)}, bf16[8,216,128]{2,1,0:T(8,128)(2,1)}, bf16[4,64,1728]{2,1,0:T(8,128)(2,1)}, f32[27,64,64]{2,1,0:T(8,128)}, f32[8,64,128]{2,1,0:T(8,128)}) custom-call(bf16[4,64,1728]{2,1,0:T(8,128)(2,1)} %feat.1, bf16[27,64,64]{2,1,0:T(8,128)(2,1)} %weight.1, bf16[8,64,128]{2,1,0:T(8,128)(2,1)} %bitcast.14, ...), custom_call_target="tpu_custom_call" | custom-call | tf_op jit(solution)/shard_map/step/pallas_call | solution.py:615
  84.9 0.0 copy-start.2
  84.9 0.0 copy-start
  84.9 2.3 %copy.26 = bf16[4,64,1728]{2,1,0:T(8,128)(2,1)} copy(bf16[4,64,1728]{2,1,0:T(8,128)(2,1)} %get-tuple-element.20) | data formatting | bytes 1769472
  87.2 0.0 copy-done.2
  87.2 0.8 copy.27
  87.9 0.0 copy-done
  87.9 0.0 copy-start.1
  87.9 0.9 %copy.28 = bf16[4,64,1728]{2,1,0:T(8,128)(2,1)} copy(bf16[4,64,1728]{2,1,0:T(8,128)(2,1)S(1)} %copy-done) | data formatting | bytes 1769472
  88.9 0.6 copy-done.1
  89.4 0.0 copy-start.3
  89.4 0.9 copy.29
  90.3 0.2 copy-done.3
  90.5 0.7 copy.30
Async XLA Ops:
  84.9 2.3 %copy-start.2 = (bf16[8,216,128]{2,1,0:T(8,128)(2,1)S(1)}, bf16[8,216,128]{2,1,0:T(8,128)(2,1)}, u32[]{:S(2)}) copy-start(bf16[8,216,128]{2,1,0:T(8,128)(2,1)} %get-tuple-element.11) | copy-start | bytes 1327108
  84.9 3.0 %copy-start = (bf16[4,64,1728]{2,1,0:T(8,128)(2,1)S(1)}, bf16[4,64,1728]{2,1,0:T(8,128)(2,1)}, u32[]{:S(2)}) copy-start(bf16[4,64,1728]{2,1,0:T(8,128)(2,1)} %get-tuple-element.22) | copy-start | bytes 2654212
  87.9 1.5 %copy-start.1 = (f32[27,64,64]{2,1,0:T(8,128)S(1)}, f32[27,64,64]{2,1,0:T(8,128)}, u32[]{:S(2)}) copy-start(f32[27,64,64]{2,1,0:T(8,128)} %get-tuple-element.23) | copy-start | bytes 1327108
  89.4 1.1 %copy-start.3 = (f32[8,64,128]{2,1,0:T(8,128)S(1)}, f32[8,64,128]{2,1,0:T(8,128)}, u32[]{:S(2)}) copy-start(f32[8,64,128]{2,1,0:T(8,128)} %get-tuple-element.14) | copy-start | bytes 786436

commit v2 on v1

--- a/solution.py
+++ b/solution.py
@@ -107,10 +107,11 @@
     return jnp.concatenate([total[ii * 64 : ii * 64 + 64] for ii in range(6)], axis=1)
 
 
-def im2col(pad_ref, b, put):
+def im2col(pad_ref, b, put, unroll=False):
     def step(ii, carry):
         for e in range(2):
-            slabs = pad_ref[b, e, pl.ds(pl.multiple_of(ii * 112, 8), 224), :]
+            start = ii * 112 if unroll else pl.multiple_of(ii * 112, 8)
+            slabs = pad_ref[b, e, pl.ds(start, 224), :]
             shifted = pltpu.roll(slabs, 223, 0)
             for a in range(3):
                 for dj in range(2):
@@ -123,7 +124,11 @@
                         put(ii, ((a * 2 + dj) * 2 + dl) * 2 + e, jnp.concatenate(pieces, axis=0).astype(BF))
         return carry
 
-    lax.fori_loop(0, 6, step, 0)
+    if unroll:
+        for ii in range(6):
+            step(ii, 0)
+    else:
+        lax.fori_loop(0, 6, step, 0)
 
 
 class Rounds:
@@ -398,16 +403,25 @@
     return out
 
 
-def step_kernel(
-    feat, weight, down, fgrad, coarse_in, send_list, recv_list, z_list, p_send, p_recv,
-    sel_in, sel_fg, sel_out, sel_up, sel_down, eye,
-    fine, coarse, grad_in, conv_out, down_out,
-    pad, cols, wide, tall, mats, fg, rows8, turned, grad_turned, kids, child, grads,
-    csend, crecv, dsend, drecv, first, second, mine, third, cs, cr, ds, dr, s1, r1, s2, r2, s3, r3, *bufs,
-):
+def step_kernel(*refs):
+    inputs, (send_list, recv_list, z_list, p_send, p_recv), refs = refs[:11], refs[11:16], refs[16:]
+    outputs, stage_in, stage_out, refs = refs[:5], refs[5:16], refs[16:21], refs[21:]
+    feat, sel_in, weight, fgrad, sel_fg, coarse_in, down, sel_up, sel_down, eye, sel_out = stage_in
+    fine, coarse, grad_in, conv_out, down_out = stage_out
+    (in_sem, out_sem, pad, cols, wide, tall, mats, fg, rows8, turned, grad_turned, kids, child, grads,
+     csend, crecv, dsend, drecv, first, second, mine, third, cs, cr, ds, dr, s1, r1, s2, r2, s3, r3, *bufs) = refs
+
+    def load(n):
+        return pltpu.make_async_copy(inputs[n], stage_in[n], in_sem.at[n])
+
+    def save(n):
+        return pltpu.make_async_copy(stage_out[n], outputs[n], out_sem.at[n])
+
     region, owner = lax.axis_index("region"), lax.axis_index("owner")
     barrier = Barrier()
     barrier.signal()
+    for n in range(11):
+        load(n).start()
     half = len(bufs) // 2
     ahead = Rounds(pad, send_list, recv_list, z_list, bufs[:half])
     back = Rounds(pad, send_list, recv_list, z_list, bufs[half:])
@@ -440,10 +454,14 @@
     def put(b, i, e, value):
         pad[b, e, (i + 1) * 56 : (i + 2) * 56, :] = value
 
+    load(0).wait()
+    load(1).wait()
     to_rows(feat, sel_in, 7, put)
     barrier.wait()
     ahead.x_start()
     kid_copies = [to_owner(csend.at[m], crecv.at[m], cs.at[m], cr.at[m], N_OWNER - m - 1) for m in range(4)]
+    for n in range(2, 11):
+        load(n).wait()
     for m in range(4):
         index = jnp.int32(0)
         for q in range(8):
@@ -475,24 +493,8 @@
             index = jnp.where(p_send[0, m] == k, m, index)
         child[k] = crecv[index]
     backward_weights(weight, tall)
-    ahead.z_end()
-
-    live = lax.rem(lax.broadcasted_iota(jnp.int32, (ROWS, 256), 0), 8) < 6
     blank = jnp.zeros((8, 128), F32)
-
-    def brick(b, carry):
-        base = pl.multiple_of(b * ROWS, 16)
-
-        def put(ii, k, value):
-            cols[pl.ds(pl.multiple_of(base + ii * 96, 16), 96), k * 128 : k * 128 + 128] = value
-
-        im2col(pad, b, put)
-        act = dot_t(cols[pl.ds(base, ROWS), :], wide[...])
-        sig = 1.0 / (1.0 + jnp.exp(-act))
-        rows = (act * sig).astype(BF)
-        for ii in range(6):
-            rows8[b, ii * 128 : ii * 128 + 96, :] = rows[ii * 96 : ii * 96 + 96]
-        slope = sig * (1.0 + act * (1.0 - sig))
+    for b in range(B):
         up = dot(sel_up[...], child[b])
         halves = [dot_t(up.astype(BF), mats[s]) for s in range(2)]
         pieces, kid = [], []
@@ -501,8 +503,26 @@
             kid += [jnp.concatenate([cut, blank], axis=1), jnp.concatenate([blank, cut], axis=1)]
             for s in range(2):
                 pieces.append(halves[s][t * 8 : t * 8 + 8])
-        kids[pl.ds(base, ROWS), :] = jnp.concatenate(kid, axis=0).astype(BF)
-        grad = (fg[b] + jnp.concatenate(pieces, axis=0)) * slope
+        kids[b * ROWS : (b + 1) * ROWS, :] = jnp.concatenate(kid, axis=0).astype(BF)
+        fg[b] = fg[b] + jnp.concatenate(pieces, axis=0)
+    ahead.z_end()
+
+    live = lax.rem(lax.broadcasted_iota(jnp.int32, (ROWS, 256), 0), 8) < 6
+
+    def brick(b, carry):
+        base = pl.multiple_of(b * ROWS, 16)
+
+        def put(ii, k, value):
+            cols[pl.ds(pl.multiple_of(base + ii * 96, 16), 96), k * 128 : k * 128 + 128] = value
+
+        im2col(pad, b, put)
+        act = dot_t(cols[pl.ds(base, ROWS), :], wide[...])
+        sig = 1.0 / (1.0 + jnp.exp(-act))
+        rows = (act * sig).astype(BF)
+        for ii in range(6):
+            rows8[b, ii * 128 : ii * 128 + 96, :] = rows[ii * 96 : ii * 96 + 96]
+        slope = sig * (1.0 + act * (1.0 - sig))
+        grad = fg[b] * slope
         grad = jnp.where(live, grad, 0.0).astype(BF)
         grad_turned[b] = dot_t(eye[...], grad).astype(BF)
         pad_rows(pad, b, grad.astype(F32))
@@ -511,22 +531,8 @@
     lax.fori_loop(0, B, brick, 0)
     back.x_start()
 
-    def contribution(b, carry):
-        pieces = [
-            dot(jnp.concatenate([rows8[b, ii * 128 : ii * 128 + 96, :] for ii in range(6)], axis=0), mats[s])
-            for s in range(2)
-        ]
-        sums = [pieces[0][t * 16 : t * 16 + 8] + pieces[1][t * 16 + 8 : t * 16 + 16] for t in range(36)]
-        coarse_tmp = dot(sel_down[...], jnp.concatenate(sums, axis=0).astype(BF)).astype(BF)
-        child[b] = coarse_tmp
+    for b in range(B):
         turned[b] = dot_t(eye[...], rows8[b]).astype(BF)
-        return carry
-
-    lax.fori_loop(0, B, contribution, 0)
-    up_copies = [to_owner(dsend.at[m], drecv.at[m], ds.at[m], dr.at[m], m + 1) for m in range(4)]
-    for m in range(4):
-        dsend[m] = child[p_send[0, m]]
-        up_copies[m].start()
 
     fold_conv(grad_turned, cols, grads)
     total = None
@@ -542,35 +548,53 @@
     each(N_OWNER, leg1, "start")
     back.x_end()
     back.y_start()
-    for b in range(2):
-        fine[b] = from_rows(turned[b], sel_out).astype(BF)
+
+    def contribution(b, carry):
+        pieces = [
+            dot(jnp.concatenate([rows8[b, ii * 128 : ii * 128 + 96, :] for ii in range(6)], axis=0), mats[s])
+            for s in range(2)
+        ]
+        sums = [pieces[0][t * 16 : t * 16 + 8] + pieces[1][t * 16 + 8 : t * 16 + 16] for t in range(36)]
+        coarse_tmp = dot(sel_down[...], jnp.concatenate(sums, axis=0).astype(BF)).astype(BF)
+        child[b] = coarse_tmp
+        return carry
+
+    lax.fori_loop(0, B, contribution, 0)
+    up_copies = [to_owner(dsend.at[m], drecv.at[m], ds.at[m], dr.at[m], m + 1) for m in range(4)]
+    for m in range(4):
+        dsend[m] = child[p_send[0, m]]
+        up_copies[m].start()
+
     back.y_end()
     back.z_start()
-    for b in range(2, B):
+    for b in range(B):
         fine[b] = from_rows(turned[b], sel_out).astype(BF)
+    save(0).start()
     for copy in up_copies:
         copy.wait_recv()
     drecv[4] = jnp.zeros((216, C2), BF)
     for q in range(8):
         coarse[q] = drecv[p_recv[0, q]]
+    save(1).start()
     back.z_end()
 
-    def back_brick(b, carry):
-        def put(ii, k, value):
-            cols[pl.ds(pl.multiple_of(ii * 96, 16), 96), k * 128 : k * 128 + 128] = value
-
-        im2col(pad, b, put)
-        rows = dot(cols[pl.ds(0, ROWS), :], tall[...]).astype(BF)
-        for ii in range(6):
-            rows8[b, ii * 128 : ii * 128 + 96, :] = rows[ii * 96 : ii * 96 + 96]
-        grad_in[b] = from_rows(dot_t(eye[...], rows8[b]).astype(BF), sel_out).astype(BF)
-        return carry
-
-    lax.fori_loop(0, 1, back_brick, 0)
     each(N_OWNER, leg1, "wait_recv")
     second[region] = lax.fori_loop(1, N_OWNER, lambda d, total: total + first[d], grads[owner])
     each(N_REGION, leg2, "start")
-    lax.fori_loop(1, 3, back_brick, 0)
+
+    def back_brick(b):
+        base = b * ROWS
+
+        def put(ii, k, value):
+            cols[base + ii * 96 : base + ii * 96 + 96, k * 128 : k * 128 + 128] = value
+
+        im2col(pad, b, put, True)
+        rows = dot(cols[base : base + ROWS, :], tall[...]).astype(BF)
+        for ii in range(6):
+            rows8[b, ii * 128 : ii * 128 + 96, :] = rows[ii * 96 : ii * 96 + 96]
+
+    back_brick(0)
+    back_brick(1)
     each(N_REGION, leg2, "wait_recv")
     part = lax.fori_loop(1, N_REGION, lambda d, total: total + second[d], second[0])
     factor = 1.0 / math.sqrt(B * N_OWNER * N_REGION * VOX)
@@ -578,7 +602,11 @@
     mine[...] = part
     each(N_OWNER, leg3, "start")
     third[owner] = part
-    lax.fori_loop(3, B, back_brick, 0)
+    back_brick(2)
+    back_brick(3)
+    for b in range(B):
+        grad_in[b] = from_rows(dot_t(eye[...], rows8[b]).astype(BF), sel_out).astype(BF)
+    save(2).start()
     each(N_OWNER, leg3, "wait_recv")
     total = third[...].astype(F32).reshape(GROWS, 128)
     for n in range(9):
@@ -589,6 +617,8 @@
         conv_out[3 * n + 2] = total[row : row + 64, (n % 2) * 64 : (n % 2) * 64 + 64]
     for t in range(8):
         down_out[t] = total[896 + t * 64 : 960 + t * 64]
+    save(3).start()
+    save(4).start()
     ahead.drain()
     back.drain()
     for copy in kid_copies + up_copies:
@@ -596,9 +626,34 @@
     each(N_OWNER, leg1, "wait_send")
     each(N_REGION, leg2, "wait_send")
     each(N_OWNER, leg3, "wait_send")
+    for n in range(5):
+        save(n).wait()
+
+
+def tail_kernel(*refs):
+    sources, results, stage, (sem_in, sem_out) = refs[:5], refs[5:10], refs[10:15], refs[15:]
+    pieces = []
+    for n in range(5):
+        size = sources[n].shape[0]
+        for k, (start, end) in enumerate(((0, size // 2), (size // 2, size))):
+            at = pl.ds(start, end - start)
+            pieces.append(
+                (
+                    pltpu.make_async_copy(sources[n].at[at], stage[n].at[at], sem_in.at[2 * n + k]),
+                    pltpu.make_async_copy(stage[n].at[at], results[n].at[at], sem_out.at[2 * n + k]),
+                )
+            )
+    for into, _ in pieces:
+        into.start()
+    for into, out in pieces:
+        into.wait()
+        out.start()
+    for _, out in pieces:
+        out.wait()
 
 
 VM = pl.BlockSpec(memory_space=pltpu.VMEM)
+ANY = pl.BlockSpec(memory_space=pl.ANY)
 SM = pl.BlockSpec(memory_space=pltpu.SMEM)
 
 
@@ -610,20 +665,28 @@
     features, conv_weight, down_weight, fine_grad, coarse_grad, face_send, face_recv, z_recv, parent_send, parent_recv
 ):
     sel_up, sel_down = coarse_selects()
-    consts = (select_in(True), select_in(False), select_out(), sel_up, sel_down, np.eye(256, dtype=np.float32).astype(BF))
+    eye = np.eye(256, dtype=np.float32).astype(BF)
+    big = (
+        features, select_in(True), conv_weight, fine_grad, select_in(False), coarse_grad[0].transpose(1, 2, 0),
+        down_weight.transpose(0, 2, 1), sel_up, sel_down, eye, select_out(),
+    )
+    big = tuple(jnp.asarray(x) for x in big)
+    results = (
+        struct((B, C, VOX), BF),
+        struct((8, 216, C2), BF),
+        struct((B, C, VOX), BF),
+        struct((27, C, C), F32),
+        struct((8, C, C2), F32),
+    )
     dma = pltpu.SemaphoreType.DMA
-    fine, coarse_out, grad_in, grad_conv, grad_down = pl.pallas_call(
+    made = pl.pallas_call(
         step_kernel,
-        out_shape=(
-            struct((B, C, VOX), BF),
-            struct((8, 216, C2), BF),
-            struct((B, C, VOX), BF),
-            struct((27, C, C), F32),
-            struct((8, C, C2), F32),
-        ),
-        in_specs=[VM] * 5 + [SM] * 5 + [VM] * 6,
-        out_specs=(VM,) * 5,
-        scratch_shapes=[
+        out_shape=results,
+        in_specs=[ANY] * 11 + [SM] * 5,
+        out_specs=(ANY,) * 5,
+        scratch_shapes=[pltpu.VMEM(x.shape, x.dtype) for x in big + results]
+        + [dma((11,)), dma((5,))]
+        + [
             pltpu.VMEM((B, 2, PROWS, 128), F32),
             pltpu.VMEM((B * ROWS, TAPS * 256), BF),
             pltpu.VMEM((256, TAPS * 256), BF),
@@ -654,10 +717,16 @@
         compiler_params=pltpu.CompilerParams(collective_id=0, has_side_effects=True, vmem_limit_bytes=VMEM_LIMIT),
         name="step",
     )(
-        features, conv_weight, down_weight.transpose(0, 2, 1), fine_grad, coarse_grad[0].transpose(1, 2, 0),
-        face_send.transpose(0, 1, 3, 2), face_recv.transpose(1, 2, 0), z_recv.transpose(1, 0), parent_send, parent_recv,
-        *(jnp.asarray(c) for c in consts),
+        *big, face_send.transpose(0, 1, 3, 2), face_recv.transpose(1, 2, 0), z_recv.transpose(1, 0), parent_send, parent_recv
     )
+    fine, coarse_out, grad_in, grad_conv, grad_down = pl.pallas_call(
+        tail_kernel,
+        out_shape=results,
+        in_specs=[ANY] * 5,
+        out_specs=(ANY,) * 5,
+        scratch_shapes=[pltpu.VMEM(x.shape, x.dtype) for x in results] + [dma((10,))] * 2,
+        name="tail",
+    )(*made)
     return fine, coarse_out.transpose(2, 0, 1)[None], grad_in, grad_conv, grad_down.transpose(0, 2, 1)
 
 

time: 91.4 us -> 82.1 us (0.90)
  local copies, waits for them, and re-layouts: 6.33 us -> 0 us
  Pallas kernels: 84.2 us -> 81.2 us
    unnamed x13 -> x0, local copies, waits for them, and re-layouts: 6.33 us -> none
    pallas_call x1 -> x2, Pallas kernels: 84.2 us -> 81.2 us  [the longest x1 78.3 us: local(): pl.pallas_call(step_kernel, out_shape=results, in_specs=[ANY] * 11 + [SM]...]
where the time goes in v2:
time: 82.1 us; the launch traced here: 82 us
  Pallas kernels  81.2 us (99%)
    pallas_call x1, Pallas kernels, local(): pl.pallas_call(step_kernel, out_shape=results, in_specs=[ANY] * 11 + [SM]...  78.3 us
    pallas_call x1, Pallas kernels, local(): pl.pallas_call(tail_kernel, out_shape=results, in_specs=[ANY] * 5, out_sp...  2.93 us

profile of v2, /device:TPU:1, one launch (start us, length us, event | category | flops | bytes accessed | tf_op | source)
XLA Modules:
  0.0 82.0 jit_solution(970709305973623877)
XLA Ops:
  0.6 78.3 %step.1 = (bf16[4,64,1728]{2,1,0:T(8,128)(2,1)}, bf16[8,216,128]{2,1,0:T(8,128)(2,1)}, bf16[4,64,1728]{2,1,0:T(8,128)(2,1)}, f32[27,64,64]{2,1,0:T(8,128)}, f32[8,64,128]{2,1,0:T(8,128)}) custom-call(bf16[4,64,1728]{2,1,0:T(8,128)(2,1)} %refs_0_.1, bf16[8,224,256]{2,1,0:T(8,128)(2,1)} %constant.12.clone.refs_1_, bf16[27,64,64]{2,1,0:T(8,128)(2,1)} %refs_2_.1, ...), custom_call_target="tpu_custom_call" | custom-call | tf_op jit(solution)/shard_map/step/pallas_call | solution.py:682
  78.9 2.9 %tail.1 = (bf16[4,64,1728]{2,1,0:T(8,128)(2,1)}, bf16[8,216,128]{2,1,0:T(8,128)(2,1)}, bf16[4,64,1728]{2,1,0:T(8,128)(2,1)}, f32[27,64,64]{2,1,0:T(8,128)}, f32[8,64,128]{2,1,0:T(8,128)}) custom-call(bf16[4,64,1728]{2,1,0:T(8,128)(2,1)} %get-tuple-element.15.refs_0_, bf16[8,216,128]{2,1,0:T(8,128)(2,1)} %get-tuple-element.16.refs_1_, ...), custom_call_target="tpu_custom_call" | custom-call | tf_op jit(solution)/shard_map/tail/pallas_call | solution.py:722

commit v3 on v2

--- a/solution.py
+++ b/solution.py
@@ -384,7 +384,7 @@
 
     def put(row, value):
         for start, size, part, at in split_rows(row, 64):
-            grads[part, at : at + size, :] = value[start : start + size]
+            grads[part, at : at + size, :] = value[start : start + size].astype(BF)
 
     for n in range(9):
         put(n * 64, main[n])
@@ -534,7 +534,6 @@
     for b in range(B):
         turned[b] = dot_t(eye[...], rows8[b]).astype(BF)
 
-    fold_conv(grad_turned, cols, grads)
     total = None
     for b in range(B):
         short = jnp.concatenate([turned[b, :, ii * 128 : ii * 128 + 96] for ii in range(6)], axis=1)
@@ -542,10 +541,23 @@
         total = part if total is None else total + part
     for s in range(2):
         for start, size, part, at in split_rows(896 + s * 256, 256):
-            grads[part, at : at + size, :] = total[start : start + size, s * 128 : s * 128 + 128]
+            grads[part, at : at + size, :] = total[start : start + size, s * 128 : s * 128 + 128].astype(BF)
     for start, size, part, at in split_rows(1408, 128):
-        grads[part, at : at + size, :] = jnp.zeros((size, 128), F32)
-    each(N_OWNER, leg1, "start")
+        grads[part, at : at + size, :] = jnp.zeros((size, 128), BF)
+    def send_parts(late):
+        def body(d, carry):
+            here = lax.rem(owner + d, N_OWNER) <= 896 // CHUNK
+
+            @pl.when(here if late else jnp.logical_not(here))
+            def _():
+                leg1(d).start()
+
+            return carry
+
+        lax.fori_loop(1, N_OWNER, body, 0)
+
+    send_parts(False)
+    fold_conv(grad_turned, cols, grads)
     back.x_end()
     back.y_start()
 
@@ -567,6 +579,7 @@
 
     back.y_end()
     back.z_start()
+    send_parts(True)
     for b in range(B):
         fine[b] = from_rows(turned[b], sel_out).astype(BF)
     save(0).start()
@@ -579,7 +592,10 @@
     back.z_end()
 
     each(N_OWNER, leg1, "wait_recv")
-    second[region] = lax.fori_loop(1, N_OWNER, lambda d, total: total + first[d], grads[owner])
+    part = grads[owner].astype(F32)
+    for d in range(1, N_OWNER):
+        part = part + first[d].astype(F32)
+    second[region] = part.astype(BF)
     each(N_REGION, leg2, "start")
 
     def back_brick(b):
@@ -596,7 +612,9 @@
     back_brick(0)
     back_brick(1)
     each(N_REGION, leg2, "wait_recv")
-    part = lax.fori_loop(1, N_REGION, lambda d, total: total + second[d], second[0])
+    part = second[0].astype(F32)
+    for d in range(1, N_REGION):
+        part = part + second[d].astype(F32)
     factor = 1.0 / math.sqrt(B * N_OWNER * N_REGION * VOX)
     part = (part * factor).astype(BF)
     mine[...] = part
@@ -698,13 +716,13 @@
             pltpu.VMEM((B, 256, ROWS), BF),
             pltpu.VMEM((B * ROWS, 256), BF),
             pltpu.VMEM((B, 216, C2), BF),
-            pltpu.VMEM((N_OWNER, CHUNK, 128), F32),
+            pltpu.VMEM((N_OWNER, CHUNK, 128), BF),
             pltpu.VMEM((4, 216, C2), BF),
             pltpu.VMEM((4, 216, C2), BF),
             pltpu.VMEM((4, 216, C2), BF),
             pltpu.VMEM((5, 216, C2), BF),
-            pltpu.VMEM((N_OWNER, CHUNK, 128), F32),
-            pltpu.VMEM((N_REGION, CHUNK, 128), F32),
+            pltpu.VMEM((N_OWNER, CHUNK, 128), BF),
+            pltpu.VMEM((N_REGION, CHUNK, 128), BF),
             pltpu.VMEM((CHUNK, 128), BF),
             pltpu.VMEM((N_OWNER, CHUNK, 128), BF),
         ]

time: 82.1 us -> 75.4 us (0.918)
  Pallas kernels: 81.2 us -> 74.5 us
    pallas_call x1, Pallas kernels: 78.3 us -> 71.5 us  [local(): pl.pallas_call(step_kernel, out_shape=results, in_specs=[ANY] * 11 + [SM]...]
where the time goes in v3:
time: 75.4 us; the launch traced here: 75.3 us
  Pallas kernels  74.5 us (99%)
  between operations  0.8 us (1%)
    pallas_call x1, Pallas kernels, local(): pl.pallas_call(step_kernel, out_shape=results, in_specs=[ANY] * 11 + [SM]...  71.5 us
    pallas_call x1, Pallas kernels, local(): pl.pallas_call(tail_kernel, out_shape=results, in_specs=[ANY] * 5, out_sp...  2.93 us

profile of v3, /device:TPU:1, one launch (start us, length us, event | category | flops | bytes accessed | tf_op | source)
XLA Modules:
  0.0 75.3 jit_solution(18079941289830671138)
XLA Ops:
  0.6 71.5 %step.1 = (bf16[4,64,1728]{2,1,0:T(8,128)(2,1)}, bf16[8,216,128]{2,1,0:T(8,128)(2,1)}, bf16[4,64,1728]{2,1,0:T(8,128)(2,1)}, f32[27,64,64]{2,1,0:T(8,128)}, f32[8,64,128]{2,1,0:T(8,128)}) custom-call(bf16[4,64,1728]{2,1,0:T(8,128)(2,1)} %refs_0_.1, bf16[8,224,256]{2,1,0:T(8,128)(2,1)} %constant.12.clone.refs_1_, bf16[27,64,64]{2,1,0:T(8,128)(2,1)} %refs_2_.1, ...), custom_call_target="tpu_custom_call" | custom-call | tf_op jit(solution)/shard_map/step/pallas_call | solution.py:700
  72.2 2.9 %tail.1 = (bf16[4,64,1728]{2,1,0:T(8,128)(2,1)}, bf16[8,216,128]{2,1,0:T(8,128)(2,1)}, bf16[4,64,1728]{2,1,0:T(8,128)(2,1)}, f32[27,64,64]{2,1,0:T(8,128)}, f32[8,64,128]{2,1,0:T(8,128)}) custom-call(bf16[4,64,1728]{2,1,0:T(8,128)(2,1)} %get-tuple-element.15.refs_0_, bf16[8,216,128]{2,1,0:T(8,128)(2,1)} %get-tuple-element.16.refs_1_, ...), custom_call_target="tpu_custom_call" | custom-call | tf_op jit(solution)/shard_map/tail/pallas_call | solution.py:740
